TPU v7x, 256 devices: a whole 4x4x8 slice. The times are simulated.
256 devices in a mesh: seq: 32 (over x, y, core), head: 8 (over z).
Axes of the slice: x: 4, y: 4, z: 8, core: 2. Of those that a mesh axis runs over, the one named last changes fastest.
Arguments:
- positions: int32 [16384], P('seq'), may hold values from 65535 to 98301, as said below
- queries: bfloat16 [16384, 32, 128], P('seq', 'head'), may hold values from -16 to 16
- keys: bfloat16 [16384, 16, 128], P('seq', 'head'), may hold values from -16 to 16
- values: bfloat16 [16384, 16, 128], P('seq', 'head'), may hold values from -6 to 6
- out_weight: bfloat16 [4096, 5376], P('head', 'seq'), may hold values from -0.1875 to 0.1875
- post_gain: float32 [5376], P('head'), may hold values from 0.25 to 1.75
- residual: bfloat16 [16384, 5376], P('seq', 'head'), may hold values from -6 to 6
Outputs:
- layer_out: bfloat16 [16384, 5376], P('seq', 'head')
Inputs may be any that keep to these rules, and one draw needn't show every extreme that they name: `positions`: strictly rising, by 1 or 2 from one token to the next; the last token's position is the most.
All inputs are finite; a program needn't handle non-finite values.
Results may differ from a plain program's by a relative error of at most 0.015.
Values may be sent and summed in bfloat16 or wider, within the bound.
No kernel may reach another device: no remote copies, remote signals or barrier semaphores. Data moves between devices by JAX's collectives and lax.ppermute only.
A program may use at most 64 MiB of HBM per device.

v0:
```python
import jax
import jax.numpy as jnp
from jax import lax
from jax.sharding import PartitionSpec as P

D = 5376
QUERY_HEADS = 32
KEY_VALUE_HEADS = 16
VISIBLE_SPAN = 1024
EPS = 1e-06
SCALE = 168.0 ** (-0.5)


def passed_along(value, axis, steps):
    count = lax.axis_size(axis)
    initial, last = (max(0, -steps), min(count, count - steps))
    return lax.ppermute(value, axis, [(source, source + steps) for source in range(initial, last)])


def copy_for_each(array, axis):
    length = lax.axis_size(axis)
    return lax.all_to_all(
        jnp.broadcast_to(array[None], (length, *array.shape)), axis, 0, 0, tiled=True
    )


def of_everyone(array, axis):
    return copy_for_each(array, axis).sum(axis=0)


def rotate(x, positions):
    half = x.shape[-1] // 2
    inverse = 10000.0 ** (-2.0 * jnp.arange(half, dtype=jnp.float32) / x.shape[-1])
    angle = positions.astype(jnp.float32)[:, None] * inverse[None, :]
    cosine = jnp.concatenate([jnp.cos(angle), jnp.cos(angle)], -1)[:, None, :]
    sine = jnp.concatenate([jnp.sin(angle), jnp.sin(angle)], -1)[:, None, :]
    source = x.astype(jnp.float32)
    turned = jnp.concatenate([-source[..., half:], source[..., :half]], -1)
    return (source * cosine + turned * sine).astype(jnp.bfloat16)


def on_device(positions, queries, keys, values, out_weight, post_gain, residual):
    rows = queries.shape[0]
    kv_heads = keys.shape[1]
    query_groups = QUERY_HEADS // KEY_VALUE_HEADS
    q_rot = rotate(queries, positions)
    stacked = jnp.stack([rotate(keys, positions), values], 0)
    reach = (VISIBLE_SPAN + rows - 2) // rows
    pieces = []
    carried = stacked
    for hop in range(reach):
        carried = passed_along(carried, "seq", 1)
        pieces.insert(0, carried)
    extended = jnp.concatenate(pieces + [stacked], axis=1)
    extra = extended.shape[1] - rows
    anchor = lax.axis_index("seq") * rows
    block_length = min(512, rows)
    query_tile_rows = q_rot.reshape(block_length, kv_heads, query_groups, -1)
    key_block = extended[0, 0 : extra + block_length]
    value_block = extended[1, 0 : extra + block_length]
    scores = (
        jnp.einsum("qhgd,khd->hgqk", query_tile_rows, key_block, preferred_element_type=jnp.float32)
        * SCALE
    )
    query_index = anchor + 0 + jnp.arange(block_length, dtype=jnp.int32)
    key_index = anchor - extra + 0 + jnp.arange(extra + block_length, dtype=jnp.int32)
    gap = query_index[:, None] - key_index[None, :]
    allowed = (gap >= 0) & (gap < VISIBLE_SPAN) & (key_index[None, :] >= 0)
    scores = jnp.where(allowed, scores, -1e30)
    top = jnp.max(scores, axis=-1, keepdims=True)
    weights = jnp.exp(scores - top)
    probs = (weights / jnp.sum(weights, axis=-1, keepdims=True)).astype(jnp.bfloat16)
    context = jnp.einsum("hgqk,khd->qhgd", probs, value_block, preferred_element_type=jnp.float32)
    outputs = context.astype(jnp.bfloat16).reshape(block_length, -1)
    context = outputs
    partial_value = jnp.dot(
        context,
        lax.all_gather(out_weight, "seq", axis=1, tiled=True),
        preferred_element_type=jnp.float32,
    )
    attended = lax.psum_scatter(
        partial_value.astype(jnp.bfloat16), "head", scatter_dimension=1, tiled=True
    ).astype(jnp.float32)
    squares = of_everyone(jnp.sum(attended * attended, axis=1), "head")
    scaled = attended * lax.rsqrt(squares / D + EPS)[:, None]
    result = residual.astype(jnp.float32) + post_gain[None, :] * scaled
    return result.astype(jnp.bfloat16)


def solution(mesh):
    return jax.shard_map(
        on_device,
        mesh=mesh,
        in_specs=(
            P("seq"),
            P("seq", "head", None),
            P("seq", "head", None),
            P("seq", "head", None),
            P("head", "seq"),
            P("head"),
            P("seq", "head"),
        ),
        out_specs=P("seq", "head"),
        check_vma=False,
    )
```

profile of v0, /device:TPU:2, one launch (start us, length us, event | category | flops | bytes accessed | tf_op | source)
XLA Modules:
  0.0 164.7 jit_solution(17591090239701363710)
XLA Ops:
  6.5 0.7 all-gather.2.cloned.1.call-update
  7.3 0.7 convert_element_type.39
  8.0 1.0 copy.44
  9.0 1.0 multiply_cosine_fusion
  10.0 0.2 pad_maximum_fusion.1
  10.2 1.0 copy_convert_fusion
  11.5 0.2 fusion.24
  11.7 0.9 pad_maximum_fusion
  12.6 1.9 %collective-permute-start = (bf16[2,512,2,128]{3,1,2,0:T(8,128)(2,1)}, bf16[2,512,2,128]{3,1,2,0:T(8,128)(2,1)}, u32[]{:S(2)}, u32[]{:S(2)}) collective-permute-start(bf16[2,512,2,128]{3,1,2,0:T(8,128)(2,1)} %pad_maximum_fusion), channel_id=1, source_target_pairs={{0,8},{8,16},{16,24},{24,32},{32,40},{40,48},{48,56},{56,64},{64,7... | collective-permute-start | bytes 1572872 | tf_op jit(solution)/shard_map/ppermute | solution.py:17
  14.8 0.6 slice_negate_fusion
  15.4 1.6 fusion.16
  17.1 8.4 %collective-permute-done = bf16[2,512,2,128]{3,1,2,0:T(8,128)(2,1)} collective-permute-done((bf16[2,512,2,128]{3,1,2,0:T(8,128)(2,1)}, bf16[2,512,2,128]{3,1,2,0:T(8,128)(2,1)}, u32[]{:S(2)}, u32[]{:S(2)}) %collective-permute-start) | collective-permute-done | bytes 524320 | tf_op jit(solution)/shard_map/ppermute | solution.py:17
  25.5 1.9 %collective-permute-start.1 = (bf16[2,512,2,128]{3,1,2,0:T(8,128)(2,1)}, bf16[2,512,2,128]{3,1,2,0:T(8,128)(2,1)S(1)}, u32[]{:S(2)}, u32[]{:S(2)}) collective-permute-start(bf16[2,512,2,128]{3,1,2,0:T(8,128)(2,1)} %collective-permute-done), channel_id=1, source_target_pairs={{0,8},{8,16},{16,24},{24,32},{32,40},{40,48},{48,56},{56,64},{64,7... | collective-permute-start | bytes 1572872 | tf_op jit(solution)/shard_map/ppermute | solution.py:17
  27.4 1.2 fusion.7
  28.6 11.5 %collective-permute-done.1 = bf16[2,512,2,128]{3,1,2,0:T(8,128)(2,1)S(1)} collective-permute-done((bf16[2,512,2,128]{3,1,2,0:T(8,128)(2,1)}, bf16[2,512,2,128]{3,1,2,0:T(8,128)(2,1)S(1)}, u32[]{:S(2)}, u32[]{:S(2)}) %collective-permute-start.1) | collective-permute-done | bytes 524320 | tf_op jit(solution)/shard_map/ppermute | solution.py:17
  40.1 1.2 maximum_maximum_fusion
  41.3 7.4 %fusion.27 = (f32[2,2,512]{2,1,0:T(2,128)S(1)}, f32[2,2,512,1536]{2,3,1,0:T(8,128)}) fusion(pred[512,1536]{0,1:T(8,128)(4,1)S(1)} %fusion.7, bf16[2,1536,2,128]{3,1,2,0:T(8,128)(2,1)S(1)} %maximum_maximum_fusion, bf16[512,2,2,128]{3,2,1,0:T(2,128)(2,1)S(1)} %bitcast.46), kind=kOutput, calls=%fused_computation.51 | convolution fusion | flops 817890816 | bytes 14688256 | tf_op jit(solution)/shard_map/sub | solution.py:71
  48.8 6.1 %fusion.14 = bf16[2,128,2,512]{3,1,2,0:T(8,128)(2,1)S(1)} fusion(f32[2,2,512,1536]{2,3,1,0:T(8,128)} %get-tuple-element.10, f32[2,2,512]{2,1,0:T(2,128)S(1)} %get-tuple-element.9, bf16[2,1536,2,128]{3,1,2,0:T(8,128)(2,1)S(1)} %maximum_maximum_fusion), kind=kOutput, calls=%fused_computation.22 | convolution fusion | flops 811859968 | bytes 13901824 | tf_op jit(solution)/shard_map/hgqk,khd->qhgd/dot_general | solution.py:73
  54.9 12.6 %all-gather.2.cloned.1.call-done = bf16[512,5376]{0,1:T(8,128)(2,1)} async-done(((bf16[512,168]{0,1:T(8,128)(2,1)}), bf16[512,5376]{0,1:T(8,128)(2,1)}) %all-gather.2.cloned.1.call-update) | async-done | bytes 5505040 | tf_op jit(solution)/shard_map/all_gather | solution.py:78
  67.4 7.3 %convolution_convert_fusion = bf16[512,5376]{0,1:T(8,128)(2,1)} fusion(bf16[512,5376]{0,1:T(8,128)(2,1)} %all-gather.2.cloned.1.call-done, bf16[512,512]{0,1:T(8,128)(2,1)S(1)} %bitcast.47), kind=kOutput, calls=%fused_computation.5 | convolution fusion | flops 2821324800 | bytes 11534336 | tf_op jit(solution)/shard_map/dot_general | solution.py:76
  74.8 67.6 %reduce-scatter.2.cloned.1.call-done = bf16[512,672]{0,1:T(8,128)(2,1)} async-done(((bf16[512,5376]{0,1:T(8,128)(2,1)}), bf16[512,672]{0,1:T(8,128)(2,1)}) %reduce-scatter.2.cloned.1.call-update) | async-done | bytes 688144 | tf_op jit(solution)/shard_map/reduce_scatter | solution.py:81
  142.4 1.3 fusion.8
  143.7 11.9 %all_to_all.6 = f32[8,1,512]{2,1,0:T(1,128)S(1)} all-to-all(f32[8,1,512]{2,1,0:T(1,128)S(1)} %broadcast_in_dim.10), channel_id=1, replica_groups=mesh['seq'=32,'head'=8] {'head'}, dimensions={0} | all-to-all | bytes 32768 | tf_op jit(solution)/shard_map/all_to_all | solution.py:22
  155.7 2.2 %fusion.11 = bf16[512,672]{0,1:T(8,128)(2,1)} fusion(bf16[512,672]{0,1:T(8,128)(2,1)} %reduce-scatter.2.cloned.1.call-done, bf16[512,672]{0,1:T(8,128)(2,1)S(1)} %copy-done.4, f32[512]{0:T(512)S(1)} %add_rsqrt_fusion, f32[672]{0:T(1024)S(1)} %copy-done.6), kind=kLoop, calls=%fused_computation.20 | loop fusion | flops 2064384 | bytes 2069120 | tf_op jit(solution)/shard_map/convert_element_type | solution.py:87
  (27 shorter events, 0.6 us)
Async XLA Ops:
  6.5 4.9 %copy-start.3 = (bf16[512,2,128]{2,1,0:T(2,128)(2,1)S(1)}, bf16[512,2,128]{2,1,0:T(2,128)(2,1)}, u32[]{:S(2)}) copy-start(bf16[512,2,128]{2,1,0:T(2,128)(2,1)} %param.9) | copy-start | bytes 786436
  6.5 60.9 %all-gather.2.cloned.1.call-start = ((), (), s32[]{:S(2)}) async-start(), calls=%async_computation.2 | async-start | bytes 5677056 | tf_op jit(solution)/shard_map/all_gather | solution.py:78
  7.3 135.1 %reduce-scatter.2.cloned.1.call-start = ((), (), s32[]{:S(2)}) async-start(), calls=%async_computation.3 | async-start | bytes 6193152 | tf_op jit(solution)/shard_map/reduce_scatter | solution.py:81
  10.2 4.3 %copy-start = (bf16[512,4,128]{2,1,0:T(4,128)(2,1)S(1)}, bf16[512,4,128]{2,1,0:T(4,128)(2,1)}, u32[]{:S(2)}) copy-start(bf16[512,4,128]{2,1,0:T(4,128)(2,1)} %param.8) | copy-start | bytes 1572868
  11.7 2.8 %copy-start.1 = (bf16[1,512,2,128]{3,1,2,0:T(8,128)(2,1)}, bf16[1,512,2,128]{3,1,2,0:T(8,128)(2,1)S(1)}, u32[]{:S(2)}) copy-start(bf16[1,512,2,128]{3,1,2,0:T(8,128)(2,1)S(1)} %fusion.24) | copy-start | bytes 786436
  12.6 12.9 %collective-permute-start = (bf16[2,512,2,128]{3,1,2,0:T(8,128)(2,1)}, bf16[2,512,2,128]{3,1,2,0:T(8,128)(2,1)}, u32[]{:S(2)}, u32[]{:S(2)}) collective-permute-start(bf16[2,512,2,128]{3,1,2,0:T(8,128)(2,1)} %pad_maximum_fusion), channel_id=1, source_target_pairs={{0,8},{8,16},{16,24},{24,32},{32,40},{40,48},{48,56},{56,64},{64,7... | collective-permute-start | bytes 1572872 | tf_op jit(solution)/shard_map/ppermute | solution.py:17
  14.8 25.3 %copy-start.2 = (bf16[1,512,2,128]{3,1,2,0:T(8,128)(2,1)S(1)}, bf16[1,512,2,128]{3,1,2,0:T(8,128)(2,1)}, u32[]{:S(2)}) copy-start(bf16[1,512,2,128]{3,1,2,0:T(8,128)(2,1)} %copy-done.1) | copy-start | bytes 786436
  17.1 24.3 %copy-start.5 = (bf16[512,4,128]{2,1,0:T(4,128)(2,1)S(1)}, bf16[512,4,128]{2,1,0:T(4,128)(2,1)}, u32[]{:S(2)}) copy-start(bf16[512,4,128]{2,1,0:T(4,128)(2,1)} %fusion.16) | copy-start | bytes 1572868
  25.5 14.7 %collective-permute-start.1 = (bf16[2,512,2,128]{3,1,2,0:T(8,128)(2,1)}, bf16[2,512,2,128]{3,1,2,0:T(8,128)(2,1)S(1)}, u32[]{:S(2)}, u32[]{:S(2)}) collective-permute-start(bf16[2,512,2,128]{3,1,2,0:T(8,128)(2,1)} %collective-permute-done), channel_id=1, source_target_pairs={{0,8},{8,16},{16,24},{24,32},{32,40},{40,48},{48,56},{56,64},{64,7... | collective-permute-start | bytes 1572872 | tf_op jit(solution)/shard_map/ppermute | solution.py:17
  74.7 80.9 %copy-start.4 = (bf16[512,672]{0,1:T(8,128)(2,1)S(1)}, bf16[512,672]{0,1:T(8,128)(2,1)}, u32[]{:S(2)}) copy-start(bf16[512,672]{0,1:T(8,128)(2,1)} %param.13) | copy-start | bytes 2064388
  74.7 80.9 %copy-start.6 = (f32[672]{0:T(1024)S(1)}, f32[672]{0:T(1024)}, u32[]{:S(2)}) copy-start(f32[672]{0:T(1024)} %param.12) | copy-start | bytes 8068
Sparse Core Ops, SparseCore 0:
  9.9 57.4 all-gather.1
  74.9 67.4 reduce-scatter.1
where the time goes:
time: 165 us
  waiting for transfers between devices  101 us (61%)
  matrix products  20.9 us (13%)
  between operations  13.6 us (8%)
  other arithmetic  12.5 us (8%)
  blocking collectives  11.9 us (7%)
  starting transfers between devices  3.86 us (2%)
    reduce_scatter x1, waiting for transfers between devices, on_device(): lax.psum_scatter(partial_value.astype(jnp.bfloat16), 'head', scatter_dime...  67.6 us
    ppermute x2, waiting for transfers between devices, passed_along(): lax.ppermute(value, axis, [(source, source + steps) for source in range(i...  19.9 us
    all_gather x1, waiting for transfers between devices, on_device(): lax.all_gather(out_weight, 'seq', axis=1, tiled=True)  12.6 us
    all_to_all x1, blocking collectives, copy_for_each(): lax.all_to_all(jnp.broadcast_to(array[None], (length, *array.shape)), axi...  11.9 us
    sub x1, matrix products, on_device(): weights = jnp.exp(scores - top)  7.44 us
    dot_general x1, matrix products, on_device(): jnp.dot(context, lax.all_gather(out_weight, 'seq', axis=1, tiled=True), p...  7.32 us
    dot_general x1, matrix products, on_device(): jnp.einsum('hgqk,khd->qhgd', probs, value_block, preferred_element_type=j...  6.11 us
    ppermute x2, starting transfers between devices, passed_along(): lax.ppermute(value, axis, [(source, source + steps) for source in range(i...  3.82 us
  transfers between devices with their start and end apart: 4, of which 4 were waited for; matrix products, arithmetic and copies ran while one was open for 14% of the time, Pallas kernels for 0%

commit v1 on v0

--- a/solution.py
+++ b/solution.py
@@ -75,7 +75,9 @@
     context = outputs
     partial_value = jnp.dot(
         context,
-        lax.all_gather(out_weight, "seq", axis=1, tiled=True),
+        jnp.concatenate(
+            lax.all_to_all(jnp.stack([out_weight] * lax.axis_size("seq")), "seq", 0, 0), axis=1
+        ),
         preferred_element_type=jnp.float32,
     )
     attended = lax.psum_scatter(

time: 165 us -> 216 us (1.31)
  waiting for transfers between devices: 101 us -> 143 us
  starting transfers between devices: 3.86 us -> 11.8 us
  local copies, waits for them, and re-layouts: 1.14 us -> 3.87 us
    ppermute x2, waiting for transfers between devices: 19.9 us -> 75.3 us  [passed_along(): lax.ppermute(value, axis, [(source, source + steps) for source in range(i...]
    all_gather x1 -> x0, waiting for transfers between devices: 12.6 us -> none  [on_device(): lax.all_gather(out_weight, 'seq', axis=1, tiled=True)]
    all_to_all x0 -> x1, starting transfers between devices: none -> 7.8 us  [on_device(): lax.all_to_all(jnp.stack([out_weight] * lax.axis_size('seq')), 'seq', 0, 0)]
    another operation x0 -> x1, local copies, waits for them, and re-layouts: none -> 3.67 us  [on_device(): jnp.stack([out_weight] * lax.axis_size('seq'))]
  transfers between devices with their start and end apart: 4 -> 4, of which waited for: 4 -> 3; matrix products, arithmetic and copies ran while one was open for 14% -> 10% of each run, Pallas kernels for 0% -> 0%
where the time goes in v1:
time: 216 us; the launch traced here: 215 us
  waiting for transfers between devices  143 us (66%)
  matrix products  20.4 us (9%)
  between operations  13.6 us (6%)
  blocking collectives  11.9 us (6%)
  starting transfers between devices  11.8 us (5%)
  other arithmetic  10.8 us (5%)
  local copies, waits for them, and re-layouts  3.87 us (2%)
    ppermute x2, waiting for transfers between devices, passed_along(): lax.ppermute(value, axis, [(source, source + steps) for source in range(i...  75.3 us
    reduce_scatter x1, waiting for transfers between devices, on_device(): lax.psum_scatter(partial_value.astype(jnp.bfloat16), 'head', scatter_dime...  67.4 us
    all_to_all x1, blocking collectives, copy_for_each(): lax.all_to_all(jnp.broadcast_to(array[None], (length, *array.shape)), axi...  11.9 us
    all_to_all x1, starting transfers between devices, on_device(): lax.all_to_all(jnp.stack([out_weight] * lax.axis_size('seq')), 'seq', 0, 0)  7.8 us
    sub x1, matrix products, on_device(): weights = jnp.exp(scores - top)  7.45 us
    dot_general x1, matrix products, on_device(): jnp.dot(context, jnp.concatenate(lax.all_to_all(jnp.stack([out_weight] *...  7.34 us
    dot_general x1, matrix products, on_device(): jnp.einsum('hgqk,khd->qhgd', probs, value_block, preferred_element_type=j...  5.66 us
  transfers between devices with their start and end apart: 4, of which 3 were waited for; matrix products, arithmetic and copies ran while one was open for 10% of the time, Pallas kernels for 0%

profile of v1, /device:TPU:2, one launch (start us, length us, event | category | flops | bytes accessed | tf_op | source)
XLA Modules:
  0.0 215.2 jit_solution(13146769772019910893)
XLA Ops:
  6.5 3.7 %stack.11 = bf16[32,512,168]{1,2,0:T(8,128)(2,1)} broadcast(bf16[512,168]{0,1:T(8,128)(2,1)} %param.11), dimensions={1,2} | broadcast | bytes 5677056 | tf_op jit(solution)/shard_map/stack | solution.py:79
  10.2 7.8 %all-to-all-start = ((bf16[32,512,168]{1,2,0:T(8,128)(2,1)}), bf16[32,512,168]{1,2,0:T(8,128)(2,1)}, u32[]{:S(2)}, u32[]{:S(2)}) async-start(bf16[32,512,168]{1,2,0:T(8,128)(2,1)} %stack.11), calls=%async_computation | async-start | bytes 11010048 | tf_op jit(solution)/shard_map/all_to_all | solution.py:79
  18.1 1.0 multiply_cosine_fusion
  19.1 0.2 pad_maximum_fusion.1
  19.4 0.2 slice_negate_fusion.1
  19.6 0.2 fusion.24
  19.9 0.9 pad_maximum_fusion
  20.7 2.0 collective-permute-start
  22.8 0.1 convert_element_type.41
  22.9 0.1 slice.29
  23.1 0.6 slice_negate_fusion
  23.7 1.6 fusion.16
  25.3 65.7 %collective-permute-done = bf16[2,512,2,128]{3,1,2,0:T(8,128)(2,1)} collective-permute-done((bf16[2,512,2,128]{3,1,2,0:T(8,128)(2,1)}, bf16[2,512,2,128]{3,1,2,0:T(8,128)(2,1)}, u32[]{:S(2)}, u32[]{:S(2)}) %collective-permute-start) | collective-permute-done | bytes 524320 | tf_op jit(solution)/shard_map/ppermute | solution.py:17
  91.0 1.9 collective-permute-start.1
  92.9 1.2 fusion.7
  94.2 9.7 %collective-permute-done.1 = bf16[2,512,2,128]{3,1,2,0:T(8,128)(2,1)S(1)} collective-permute-done((bf16[2,512,2,128]{3,1,2,0:T(8,128)(2,1)}, bf16[2,512,2,128]{3,1,2,0:T(8,128)(2,1)S(1)}, u32[]{:S(2)}, u32[]{:S(2)}) %collective-permute-start.1) | collective-permute-done | bytes 524320 | tf_op jit(solution)/shard_map/ppermute | solution.py:17
  103.8 1.2 maximum_maximum_fusion
  105.0 7.4 %fusion.27 = (f32[2,2,512]{2,1,0:T(2,128)S(1)}, f32[2,2,512,1536]{2,3,1,0:T(8,128)}) fusion(pred[512,1536]{0,1:T(8,128)(4,1)S(1)} %fusion.7, bf16[2,1536,2,128]{3,1,2,0:T(8,128)(2,1)S(1)} %maximum_maximum_fusion, bf16[512,2,2,128]{3,2,1,0:T(2,128)(2,1)S(1)} %bitcast.49), kind=kOutput, calls=%fused_computation.51 | convolution fusion | flops 817890816 | bytes 14688256 | tf_op jit(solution)/shard_map/sub | solution.py:71
  112.4 5.7 %fusion.14 = bf16[2,128,2,512]{3,1,2,0:T(8,128)(2,1)S(1)} fusion(f32[2,2,512,1536]{2,3,1,0:T(8,128)} %get-tuple-element.10, f32[2,2,512]{2,1,0:T(2,128)S(1)} %get-tuple-element.9, bf16[2,1536,2,128]{3,1,2,0:T(8,128)(2,1)S(1)} %maximum_maximum_fusion), kind=kOutput, calls=%fused_computation.22 | convolution fusion | flops 811859968 | bytes 13901824 | tf_op jit(solution)/shard_map/hgqk,khd->qhgd/dot_general | solution.py:73
  118.1 7.3 %convolution_convert_fusion = bf16[512,5376]{0,1:T(8,128)(2,1)} fusion(bf16[512,5376]{0,1:T(8,128)(2,1)} %bitcast.12, bf16[512,512]{0,1:T(8,128)(2,1)S(1)} %bitcast.50), kind=kOutput, calls=%fused_computation.5 | convolution fusion | flops 2821324800 | bytes 11534336 | tf_op jit(solution)/shard_map/dot_general | solution.py:76
  125.5 67.4 %reduce-scatter.2.cloned.1.call-done = bf16[512,672]{0,1:T(8,128)(2,1)} async-done(((bf16[512,5376]{0,1:T(8,128)(2,1)}), bf16[512,672]{0,1:T(8,128)(2,1)}) %reduce-scatter.2.cloned.1.call-update) | async-done | bytes 688144 | tf_op jit(solution)/shard_map/reduce_scatter | solution.py:83
  192.9 1.3 fusion.8
  194.2 11.9 %all_to_all.11 = f32[8,1,512]{2,1,0:T(1,128)S(1)} all-to-all(f32[8,1,512]{2,1,0:T(1,128)S(1)} %broadcast_in_dim.10), channel_id=1, replica_groups=mesh['seq'=32,'head'=8] {'head'}, dimensions={0} | all-to-all | bytes 32768 | tf_op jit(solution)/shard_map/all_to_all | solution.py:22
  206.2 2.2 %fusion.11 = bf16[512,672]{0,1:T(8,128)(2,1)} fusion(bf16[512,672]{0,1:T(8,128)(2,1)} %reduce-scatter.2.cloned.1.call-done, bf16[512,672]{0,1:T(8,128)(2,1)S(1)} %copy-done.4, f32[512]{0:T(512)S(1)} %add_rsqrt_fusion, f32[672]{0:T(1024)S(1)} %copy-done.7), kind=kLoop, calls=%fused_computation.20 | loop fusion | flops 2064384 | bytes 2069120 | tf_op jit(solution)/shard_map/convert_element_type | solution.py:89
  (31 shorter events, 0.3 us)
Async XLA Ops:
  10.2 7.9 %copy-start.8 = (s32[512]{0:T(512)S(1)}, s32[512]{0:T(512)}, u32[]{:S(2)}) copy-start(s32[512]{0:T(512)} %param.7) | copy-start | bytes 6148
  10.2 8.9 %copy-start.6 = (bf16[512,2,128]{2,1,0:T(2,128)(2,1)S(1)}, bf16[512,2,128]{2,1,0:T(2,128)(2,1)}, u32[]{:S(2)}) copy-start(bf16[512,2,128]{2,1,0:T(2,128)(2,1)} %param.10) | copy-start | bytes 786436
  10.2 9.1 %copy-start.3 = (bf16[512,2,128]{2,1,0:T(2,128)(2,1)S(1)}, bf16[512,2,128]{2,1,0:T(2,128)(2,1)}, u32[]{:S(2)}) copy-start(bf16[512,2,128]{2,1,0:T(2,128)(2,1)} %param.9) | copy-start | bytes 786436
  10.2 107.9 %all-to-all-start = ((bf16[32,512,168]{1,2,0:T(8,128)(2,1)}), bf16[32,512,168]{1,2,0:T(8,128)(2,1)}, u32[]{:S(2)}, u32[]{:S(2)}) async-start(bf16[32,512,168]{1,2,0:T(8,128)(2,1)} %stack.11), calls=%async_computation | async-start | bytes 11010048 | tf_op jit(solution)/shard_map/all_to_all | solution.py:79
  18.0 174.9 %reduce-scatter.2.cloned.1.call-start = ((), (), s32[]{:S(2)}) async-start(), calls=%async_computation.3 | async-start | bytes 6193152 | tf_op jit(solution)/shard_map/reduce_scatter | solution.py:83
  19.4 3.4 %copy-start = (bf16[512,4,128]{2,1,0:T(4,128)(2,1)S(1)}, bf16[512,4,128]{2,1,0:T(4,128)(2,1)}, u32[]{:S(2)}) copy-start(bf16[512,4,128]{2,1,0:T(4,128)(2,1)} %param.8) | copy-start | bytes 1572868
  19.9 2.9 %copy-start.1 = (bf16[1,512,2,128]{3,1,2,0:T(8,128)(2,1)}, bf16[1,512,2,128]{3,1,2,0:T(8,128)(2,1)S(1)}, u32[]{:S(2)}) copy-start(bf16[1,512,2,128]{3,1,2,0:T(8,128)(2,1)S(1)} %fusion.24) | copy-start | bytes 786436
  20.7 70.3 %collective-permute-start = (bf16[2,512,2,128]{3,1,2,0:T(8,128)(2,1)}, bf16[2,512,2,128]{3,1,2,0:T(8,128)(2,1)}, u32[]{:S(2)}, u32[]{:S(2)}) collective-permute-start(bf16[2,512,2,128]{3,1,2,0:T(8,128)(2,1)} %pad_maximum_fusion), channel_id=1, source_target_pairs={{0,8},{8,16},{16,24},{24,32},{32,40},{40,48},{48,56},{56,64},{64,7... | collective-permute-start | bytes 1572872 | tf_op jit(solution)/shard_map/ppermute | solution.py:17
  23.1 80.7 %copy-start.2 = (bf16[1,512,2,128]{3,1,2,0:T(8,128)(2,1)S(1)}, bf16[1,512,2,128]{3,1,2,0:T(8,128)(2,1)}, u32[]{:S(2)}) copy-start(bf16[1,512,2,128]{3,1,2,0:T(8,128)(2,1)} %copy-done.1) | copy-start | bytes 786436
  25.3 79.7 %copy-start.5 = (bf16[512,4,128]{2,1,0:T(4,128)(2,1)S(1)}, bf16[512,4,128]{2,1,0:T(4,128)(2,1)}, u32[]{:S(2)}) copy-start(bf16[512,4,128]{2,1,0:T(4,128)(2,1)} %fusion.16) | copy-start | bytes 1572868
  91.0 12.8 %collective-permute-start.1 = (bf16[2,512,2,128]{3,1,2,0:T(8,128)(2,1)}, bf16[2,512,2,128]{3,1,2,0:T(8,128)(2,1)S(1)}, u32[]{:S(2)}, u32[]{:S(2)}) collective-permute-start(bf16[2,512,2,128]{3,1,2,0:T(8,128)(2,1)} %collective-permute-done), channel_id=1, source_target_pairs={{0,8},{8,16},{16,24},{24,32},{32,40},{40,48},{48,56},{56,64},{64,7... | collective-permute-start | bytes 1572872 | tf_op jit(solution)/shard_map/ppermute | solution.py:17
  125.5 80.7 %copy-start.4 = (bf16[512,672]{0,1:T(8,128)(2,1)S(1)}, bf16[512,672]{0,1:T(8,128)(2,1)}, u32[]{:S(2)}) copy-start(bf16[512,672]{0,1:T(8,128)(2,1)} %param.13) | copy-start | bytes 2064388
  125.5 80.7 %copy-start.7 = (f32[672]{0:T(1024)S(1)}, f32[672]{0:T(1024)}, u32[]{:S(2)}) copy-start(f32[672]{0:T(1024)} %param.12) | copy-start | bytes 8068
Sparse Core Ops, SparseCore 0:
  125.6 67.2 reduce-scatter.1
